TPU v7x, 32 devices: a whole 2x2x4 slice. The times are simulated.
32 devices in a mesh: db: 8 (over y, x, core), pb: 4 (over z).
Axes of the slice: x: 2, y: 2, z: 4, core: 2. Of those that a mesh axis runs over, the one named last changes fastest.
Arguments:
- query_maps: bfloat16 [32, 256, 256], P(('db', 'pb')), may hold values from -6 to 6
- database: bfloat16 [1024, 256, 256], P(('db', 'pb')), may hold values from -6 to 6
- shortlist: int32 [32, 128], P(('db', 'pb')), may hold values from 0 to 1023, as said below
- kernel_query: bfloat16 [3, 3], replicated, may hold values from -1.5 to 1.5
- kernel_db: bfloat16 [3, 3], replicated, may hold values from -1.5 to 1.5
Outputs:
- scores: float32 [32, 128], P(('db', 'pb'))
- top_scores: float32 [32, 100], P(('db', 'pb'))
Inputs may be any that keep to these rules, and one draw needn't show every extreme that they name: Within one query the ids are distinct. Among the 128 shortlist entries of the query held by device q (query q), at most 8 lie in any one shard of images (ids s * 32 to (s + 1) * 32 - 1), and some shard holds exactly 8 of them for every device.
All inputs are finite; a program needn't handle non-finite values.
Results may differ from a plain program's by a relative error of at most 0.0003.
Values may be sent and summed in bfloat16 or wider, within the bound.
A program may use at most 128 MiB of HBM per device.

v0:
```python
import math
import jax
import jax.numpy as jnp
from jax import lax
from jax.sharding import PartitionSpec as P

GRID = 16
TOPK = 100
epsilon = 1e-06
score_scale = 8.0


def unit_maps(maps):
    values = maps.astype(jnp.float32)
    squares = jnp.sum(values * values, axis=1, keepdims=True)
    return (values * lax.rsqrt(squares + epsilon)).astype(jnp.bfloat16)


def conv_matrix(kernel):
    cell_count = GRID * GRID
    cell_index = jnp.arange(cell_count)
    row_out = (cell_index // GRID)[:, None]
    col_out = (cell_index % GRID)[:, None]
    row_in = (cell_index // GRID)[None, :]
    col_in = (cell_index % GRID)[None, :]
    weights = kernel.astype(jnp.float32)
    matrix = jnp.zeros((cell_count, cell_count), jnp.float32)
    for i in range(3):
        for j in range(3):
            hit = (row_in == row_out + i - 1) & (col_in == col_out + j - 1)
            matrix = matrix + weights[i, j] * hit.astype(jnp.float32)
    return matrix.astype(jnp.bfloat16)


def finish_pairs(correlation, conv_query, conv_db):
    rectified = jnp.maximum(correlation, 0.0).astype(jnp.bfloat16)
    filtered = jnp.einsum("qa,nab->nqb", conv_query, rectified, preferred_element_type=jnp.float32)
    filtered = filtered + jnp.einsum(
        "nqa,ba->nqb", rectified, conv_db, preferred_element_type=jnp.float32
    )
    return score_scale * jnp.mean(jnp.max(filtered, axis=1), axis=-1)


def shard_scores(gathered, slots, db_unit, conv_query, conv_db):
    source_count, width = slots.shape
    per_query = gathered.shape[0] // source_count
    grouped = gathered.reshape(source_count, per_query, gathered.shape[1], gathered.shape[2])
    step_size = math.gcd(source_count, max(1, 32 // width))

    def score_block(start):
        slot_block = lax.dynamic_slice_in_dim(slots, start, step_size, 0)
        group_block = lax.dynamic_slice_in_dim(grouped, start, step_size, 0)
        images = db_unit[slot_block]
        correlation = jnp.einsum(
            "scq,skcd->skqd", group_block[:, 0], images, preferred_element_type=jnp.float32
        )
        correlation = correlation.reshape(
            step_size * width, correlation.shape[-2], correlation.shape[-1]
        )
        return finish_pairs(correlation, conv_query, conv_db)

    starts = jnp.arange(source_count // step_size, dtype=jnp.int32) * step_size
    return lax.map(score_block, starts).reshape(source_count, width)


def body(query_maps, database, shortlist, kernel_query, kernel_db):
    query_unit = unit_maps(query_maps)
    db_unit = unit_maps(database)
    conv_query = conv_matrix(kernel_query)
    conv_db = conv_matrix(kernel_db)
    db_count = lax.axis_size("db")
    pb_count = lax.axis_size("pb")
    shard_count = db_count * pb_count
    per_query = query_maps.shape[0]
    cand_count = shortlist.shape[1]
    image_count = database.shape[0]
    flat_ids = shortlist.reshape(-1)
    row_count = flat_ids.shape[0]
    capacity = 2 * row_count // shard_count
    shard_of = flat_ids // image_count
    slot_of = flat_ids % image_count
    one_hot = (shard_of[:, None] == jnp.arange(shard_count, dtype=jnp.int32)[None, :]).astype(
        jnp.int32
    )
    bucket_pos = jnp.sum(jnp.cumsum(one_hot, axis=0) * one_hot, axis=1) - 1
    row_ids = jnp.arange(row_count, dtype=jnp.int32)
    query_of = row_ids // cand_count
    empty = jnp.zeros((shard_count, capacity), jnp.int32)
    send_slot = empty.at[shard_of, bucket_pos].set(slot_of)
    send_query = empty.at[shard_of, bucket_pos].set(query_of)
    requests = jnp.stack([send_slot, send_query])
    gathered = lax.all_gather(query_unit, ("db", "pb"), axis=0, tiled=True)
    found = shard_scores(
        gathered,
        lax.all_to_all(requests, ("db", "pb"), split_axis=1, concat_axis=1, tiled=True)[0],
        db_unit,
        conv_query,
        conv_db,
    )
    returned = lax.all_to_all(found, ("db", "pb"), split_axis=0, concat_axis=0, tiled=True)
    scores = returned[shard_of, bucket_pos].reshape(per_query, cand_count)
    top_scores = lax.top_k(scores, TOPK)[0]
    return (scores, top_scores)


def solution(mesh):
    in_specs = (
        P(("db", "pb"), None, None),
        P(("db", "pb"), None, None),
        P(("db", "pb"), None),
        P(),
        P(),
    )
    out_specs = (P(("db", "pb"), None), P(("db", "pb"), None))
    return jax.shard_map(body, mesh=mesh, in_specs=in_specs, out_specs=out_specs, check_vma=False)
```

profile of v0, /device:TPU:0, one launch (start us, length us, event | category | flops | bytes accessed | tf_op | source)
XLA Modules:
  0.0 317.0 jit_solution(1332410492687568349)
XLA Ops:
  7.2 1.0 fusion.53
  8.2 1.6 fusion.54
  9.8 0.7 and_select_fusion.3
  10.5 0.2 reduce_window_sum.11
  10.7 0.2 select_reduce_fusion
  10.9 0.7 fusion.61
  11.6 6.4 %scatter_fusion = s32[32,8]{0,1:T(8,128)S(1)} fusion(s32[32,8]{0,1:T(8,128)S(1)} %broadcast_in_dim.11.clone.1, s32[128]{0:T(128)S(1)} %fusion.60, s32[128]{0:T(128)S(1)} %get-tuple-element.427), kind=kCustom, calls=%fused_computation.2 | custom fusion | bytes 2560 | tf_op jit(solution)/shard_map/scatter | solution.py:89
  18.1 6.4 %scatter_fusion.1 = s32[32,8]{0,1:T(8,128)S(1)} fusion(s32[32,8]{0,1:T(8,128)S(1)} %broadcast_in_dim.11.clone, s32[128]{0:T(128)S(1)} %fusion.60, s32[128]{0:T(128)S(1)} %and_select_fusion.2), kind=kCustom, calls=%fused_computation.3 | custom fusion | bytes 2560 | tf_op jit(solution)/shard_map/scatter | solution.py:90
  24.5 0.7 copy.23
  25.2 7.3 %all-to-all-start = ((s32[2,32,8]{2,0,1:T(2,128)}), s32[2,32,8]{2,0,1:T(2,128)S(1)}, u32[]{:S(2)}, u32[]{:S(2)}) async-start(s32[2,32,8]{2,0,1:T(2,128)} %copy.23), calls=%async_computation | async-start | bytes 65536 | tf_op jit(solution)/shard_map/all_to_all | solution.py:95
  32.6 1.7 fusion.63
  34.3 1.7 fusion.62
  36.0 3.1 fusion.51
  39.1 3.1 fusion.52
  42.2 33.2 %all-gather.2.cloned.1.call-done = bf16[32,256,256]{2,1,0:T(8,128)(2,1)} async-done(((bf16[1,256,256]{2,1,0:T(8,128)(2,1)}), bf16[32,256,256]{2,1,0:T(8,128)(2,1)}) %all-gather.2.cloned.1.call-update) | async-done | bytes 4194320 | tf_op jit(solution)/shard_map/all_gather | solution.py:92
  75.4 220.3 %while.14 = (s32[]{:T(128)}, f32[8,32]{1,0:T(8,128)S(1)}, s32[8]{0:T(128)S(1)}, s32[32,8]{1,0:T(8,128)S(1)}, bf16[32,256,256]{2,1,0:T(8,128)(2,1)}, /*index=5*/b...) while((s32[]{:T(128)}, f32[8,32]{1,0:T(8,128)S(1)}, ...), condition=%wide.region_9.10_spmd.clone.clone, body=%wide.region_6.9_spmd.clone.clone.sunk | while | flops 3233940480 | bytes 42551080 | solution.py:63
  75.4 0.6 dynamic_slice.35
  77.8 5.0 %gather_fusion = bf16[32,256,256]{2,1,0:T(8,128)(2,1)} fusion(bf16[32,256,256]{2,1,0:T(8,128)(2,1)} %get-tuple-element.688, s32[1024]{0:T(1024)S(1)} %pad_clamp_fusion.2), kind=kCustom, calls=%fused_computation.clone.clone.clone.1 | custom fusion | bytes 8388736 | tf_op jit(solution)/shard_map/while/body/eval_jaxpr/gather | solution.py:53
  82.7 4.0 %maximum_convert_fusion.2 = bf16[4,8,256,256]{3,2,1,0:T(8,128)(2,1)S(1)} fusion(bf16[4,8,256,256]{3,2,1,0:T(8,128)(2,1)} %bitcast.126, bf16[32,1,256,256]{3,2,0,1:T(8,128)(2,1)} %get-tuple-element.689, s32[]{:T(128)S(6)} %select_n.224), kind=kOutput, calls=%fused_computation.8.clone.1 | convolution fusion | flops 1077936128 | bytes 8912900 | tf_op jit(solution)/shard_map/while/body/eval_jaxpr/scq,skcd->skqd/dot_general | solution.py:54
  86.8 7.3 %fusion.81 = f32[32,256,256]{1,2,0:T(8,128)S(1)} fusion(bf16[32,256,256]{1,2,0:T(8,128)(2,1)S(1)} %bitcast.124, f32[]{:T(128)} %get-tuple-element.704, f32[]{:T(128)} %get-tuple-element.701, f32[]{:T(128)} %get-tuple-element.699, f32[]{:T(128)} %get-tuple-element.697, f32[]{:T(128)} %get-tuple-element.695, f32[]{:T(128)} %get-tuple-element.694, ...), kind=kOutput, calls=%fused_computation.23.clone.1 | convolution fusion | flops 1075904512 | bytes 12589092 | tf_op jit(solution)/shard_map/while/body/eval_jaxpr/qa,nab->nqb/dot_general | solution.py:37
  94.1 8.6 %fusion.82 = f32[32,256]{1,0:T(8,128)S(1)} fusion(f32[32,256,256]{1,2,0:T(8,128)S(1)} %fusion.81, bf16[32,256,256]{1,2,0:T(8,128)(2,1)S(1)} %bitcast.125, f32[]{:T(128)} %get-tuple-element.713, f32[]{:T(128)} %get-tuple-element.712, f32[]{:T(128)} %get-tuple-element.711, f32[]{:T(128)} %get-tuple-element.710, f32[]{:T(128)} %get-tuple-element.709, ...), kind=kOutput, calls=%fused_computation.7.clone.1 | convolution fusion | flops 1080090624 | bytes 12621860 | tf_op jit(solution)/shard_map/while/body/eval_jaxpr/nqa,ba->nqb/dot_general | solution.py:38
  102.7 0.1 reduce_sum.48
  102.9 0.6 dynamic_slice.35
  105.3 5.0 %gather_fusion = bf16[32,256,256]{2,1,0:T(8,128)(2,1)} fusion(bf16[32,256,256]{2,1,0:T(8,128)(2,1)} %get-tuple-element.688, s32[1024]{0:T(1024)S(1)} %pad_clamp_fusion.2), kind=kCustom, calls=%fused_computation.clone.clone.clone.1 | custom fusion | bytes 8388736 | tf_op jit(solution)/shard_map/while/body/eval_jaxpr/gather | solution.py:53
  110.3 4.0 %maximum_convert_fusion.2 = bf16[4,8,256,256]{3,2,1,0:T(8,128)(2,1)S(1)} fusion(bf16[4,8,256,256]{3,2,1,0:T(8,128)(2,1)} %bitcast.126, bf16[32,1,256,256]{3,2,0,1:T(8,128)(2,1)} %get-tuple-element.689, s32[]{:T(128)S(6)} %select_n.224), kind=kOutput, calls=%fused_computation.8.clone.1 | convolution fusion | flops 1077936128 | bytes 8912900 | tf_op jit(solution)/shard_map/while/body/eval_jaxpr/scq,skcd->skqd/dot_general | solution.py:54
  114.3 7.3 %fusion.81 = f32[32,256,256]{1,2,0:T(8,128)S(1)} fusion(bf16[32,256,256]{1,2,0:T(8,128)(2,1)S(1)} %bitcast.124, f32[]{:T(128)} %get-tuple-element.704, f32[]{:T(128)} %get-tuple-element.701, f32[]{:T(128)} %get-tuple-element.699, f32[]{:T(128)} %get-tuple-element.697, f32[]{:T(128)} %get-tuple-element.695, f32[]{:T(128)} %get-tuple-element.694, ...), kind=kOutput, calls=%fused_computation.23.clone.1 | convolution fusion | flops 1075904512 | bytes 12589092 | tf_op jit(solution)/shard_map/while/body/eval_jaxpr/qa,nab->nqb/dot_general | solution.py:37
  121.6 8.6 %fusion.82 = f32[32,256]{1,0:T(8,128)S(1)} fusion(f32[32,256,256]{1,2,0:T(8,128)S(1)} %fusion.81, bf16[32,256,256]{1,2,0:T(8,128)(2,1)S(1)} %bitcast.125, f32[]{:T(128)} %get-tuple-element.713, f32[]{:T(128)} %get-tuple-element.712, f32[]{:T(128)} %get-tuple-element.711, f32[]{:T(128)} %get-tuple-element.710, f32[]{:T(128)} %get-tuple-element.709, ...), kind=kOutput, calls=%fused_computation.7.clone.1 | convolution fusion | flops 1080090624 | bytes 12621860 | tf_op jit(solution)/shard_map/while/body/eval_jaxpr/nqa,ba->nqb/dot_general | solution.py:38
  130.3 0.1 reduce_sum.48
  130.5 0.6 dynamic_slice.35
  132.8 5.0 %gather_fusion = bf16[32,256,256]{2,1,0:T(8,128)(2,1)} fusion(bf16[32,256,256]{2,1,0:T(8,128)(2,1)} %get-tuple-element.688, s32[1024]{0:T(1024)S(1)} %pad_clamp_fusion.2), kind=kCustom, calls=%fused_computation.clone.clone.clone.1 | custom fusion | bytes 8388736 | tf_op jit(solution)/shard_map/while/body/eval_jaxpr/gather | solution.py:53
  137.8 4.0 %maximum_convert_fusion.2 = bf16[4,8,256,256]{3,2,1,0:T(8,128)(2,1)S(1)} fusion(bf16[4,8,256,256]{3,2,1,0:T(8,128)(2,1)} %bitcast.126, bf16[32,1,256,256]{3,2,0,1:T(8,128)(2,1)} %get-tuple-element.689, s32[]{:T(128)S(6)} %select_n.224), kind=kOutput, calls=%fused_computation.8.clone.1 | convolution fusion | flops 1077936128 | bytes 8912900 | tf_op jit(solution)/shard_map/while/body/eval_jaxpr/scq,skcd->skqd/dot_general | solution.py:54
  141.8 7.3 %fusion.81 = f32[32,256,256]{1,2,0:T(8,128)S(1)} fusion(bf16[32,256,256]{1,2,0:T(8,128)(2,1)S(1)} %bitcast.124, f32[]{:T(128)} %get-tuple-element.704, f32[]{:T(128)} %get-tuple-element.701, f32[]{:T(128)} %get-tuple-element.699, f32[]{:T(128)} %get-tuple-element.697, f32[]{:T(128)} %get-tuple-element.695, f32[]{:T(128)} %get-tuple-element.694, ...), kind=kOutput, calls=%fused_computation.23.clone.1 | convolution fusion | flops 1075904512 | bytes 12589092 | tf_op jit(solution)/shard_map/while/body/eval_jaxpr/qa,nab->nqb/dot_general | solution.py:37
  149.2 8.6 %fusion.82 = f32[32,256]{1,0:T(8,128)S(1)} fusion(f32[32,256,256]{1,2,0:T(8,128)S(1)} %fusion.81, bf16[32,256,256]{1,2,0:T(8,128)(2,1)S(1)} %bitcast.125, f32[]{:T(128)} %get-tuple-element.713, f32[]{:T(128)} %get-tuple-element.712, f32[]{:T(128)} %get-tuple-element.711, f32[]{:T(128)} %get-tuple-element.710, f32[]{:T(128)} %get-tuple-element.709, ...), kind=kOutput, calls=%fused_computation.7.clone.1 | convolution fusion | flops 1080090624 | bytes 12621860 | tf_op jit(solution)/shard_map/while/body/eval_jaxpr/nqa,ba->nqb/dot_general | solution.py:38
  157.8 0.1 reduce_sum.48
  158.0 0.6 dynamic_slice.35
  160.4 5.0 %gather_fusion = bf16[32,256,256]{2,1,0:T(8,128)(2,1)} fusion(bf16[32,256,256]{2,1,0:T(8,128)(2,1)} %get-tuple-element.688, s32[1024]{0:T(1024)S(1)} %pad_clamp_fusion.2), kind=kCustom, calls=%fused_computation.clone.clone.clone.1 | custom fusion | bytes 8388736 | tf_op jit(solution)/shard_map/while/body/eval_jaxpr/gather | solution.py:53
  165.4 4.0 %maximum_convert_fusion.2 = bf16[4,8,256,256]{3,2,1,0:T(8,128)(2,1)S(1)} fusion(bf16[4,8,256,256]{3,2,1,0:T(8,128)(2,1)} %bitcast.126, bf16[32,1,256,256]{3,2,0,1:T(8,128)(2,1)} %get-tuple-element.689, s32[]{:T(128)S(6)} %select_n.224), kind=kOutput, calls=%fused_computation.8.clone.1 | convolution fusion | flops 1077936128 | bytes 8912900 | tf_op jit(solution)/shard_map/while/body/eval_jaxpr/scq,skcd->skqd/dot_general | solution.py:54
  169.4 7.3 %fusion.81 = f32[32,256,256]{1,2,0:T(8,128)S(1)} fusion(bf16[32,256,256]{1,2,0:T(8,128)(2,1)S(1)} %bitcast.124, f32[]{:T(128)} %get-tuple-element.704, f32[]{:T(128)} %get-tuple-element.701, f32[]{:T(128)} %get-tuple-element.699, f32[]{:T(128)} %get-tuple-element.697, f32[]{:T(128)} %get-tuple-element.695, f32[]{:T(128)} %get-tuple-element.694, ...), kind=kOutput, calls=%fused_computation.23.clone.1 | convolution fusion | flops 1075904512 | bytes 12589092 | tf_op jit(solution)/shard_map/while/body/eval_jaxpr/qa,nab->nqb/dot_general | solution.py:37
  176.7 8.6 %fusion.82 = f32[32,256]{1,0:T(8,128)S(1)} fusion(f32[32,256,256]{1,2,0:T(8,128)S(1)} %fusion.81, bf16[32,256,256]{1,2,0:T(8,128)(2,1)S(1)} %bitcast.125, f32[]{:T(128)} %get-tuple-element.713, f32[]{:T(128)} %get-tuple-element.712, f32[]{:T(128)} %get-tuple-element.711, f32[]{:T(128)} %get-tuple-element.710, f32[]{:T(128)} %get-tuple-element.709, ...), kind=kOutput, calls=%fused_computation.7.clone.1 | convolution fusion | flops 1080090624 | bytes 12621860 | tf_op jit(solution)/shard_map/while/body/eval_jaxpr/nqa,ba->nqb/dot_general | solution.py:38
  185.4 0.1 reduce_sum.48
  185.6 0.6 dynamic_slice.35
  187.9 5.0 %gather_fusion = bf16[32,256,256]{2,1,0:T(8,128)(2,1)} fusion(bf16[32,256,256]{2,1,0:T(8,128)(2,1)} %get-tuple-element.688, s32[1024]{0:T(1024)S(1)} %pad_clamp_fusion.2), kind=kCustom, calls=%fused_computation.clone.clone.clone.1 | custom fusion | bytes 8388736 | tf_op jit(solution)/shard_map/while/body/eval_jaxpr/gather | solution.py:53
  192.9 4.0 %maximum_convert_fusion.2 = bf16[4,8,256,256]{3,2,1,0:T(8,128)(2,1)S(1)} fusion(bf16[4,8,256,256]{3,2,1,0:T(8,128)(2,1)} %bitcast.126, bf16[32,1,256,256]{3,2,0,1:T(8,128)(2,1)} %get-tuple-element.689, s32[]{:T(128)S(6)} %select_n.224), kind=kOutput, calls=%fused_computation.8.clone.1 | convolution fusion | flops 1077936128 | bytes 8912900 | tf_op jit(solution)/shard_map/while/body/eval_jaxpr/scq,skcd->skqd/dot_general | solution.py:54
  196.9 7.3 %fusion.81 = f32[32,256,256]{1,2,0:T(8,128)S(1)} fusion(bf16[32,256,256]{1,2,0:T(8,128)(2,1)S(1)} %bitcast.124, f32[]{:T(128)} %get-tuple-element.704, f32[]{:T(128)} %get-tuple-element.701, f32[]{:T(128)} %get-tuple-element.699, f32[]{:T(128)} %get-tuple-element.697, f32[]{:T(128)} %get-tuple-element.695, f32[]{:T(128)} %get-tuple-element.694, ...), kind=kOutput, calls=%fused_computation.23.clone.1 | convolution fusion | flops 1075904512 | bytes 12589092 | tf_op jit(solution)/shard_map/while/body/eval_jaxpr/qa,nab->nqb/dot_general | solution.py:37
  204.3 8.6 %fusion.82 = f32[32,256]{1,0:T(8,128)S(1)} fusion(f32[32,256,256]{1,2,0:T(8,128)S(1)} %fusion.81, bf16[32,256,256]{1,2,0:T(8,128)(2,1)S(1)} %bitcast.125, f32[]{:T(128)} %get-tuple-element.713, f32[]{:T(128)} %get-tuple-element.712, f32[]{:T(128)} %get-tuple-element.711, f32[]{:T(128)} %get-tuple-element.710, f32[]{:T(128)} %get-tuple-element.709, ...), kind=kOutput, calls=%fused_computation.7.clone.1 | convolution fusion | flops 1080090624 | bytes 12621860 | tf_op jit(solution)/shard_map/while/body/eval_jaxpr/nqa,ba->nqb/dot_general | solution.py:38
  213.1 0.6 dynamic_slice.35
  215.5 5.0 %gather_fusion = bf16[32,256,256]{2,1,0:T(8,128)(2,1)} fusion(bf16[32,256,256]{2,1,0:T(8,128)(2,1)} %get-tuple-element.688, s32[1024]{0:T(1024)S(1)} %pad_clamp_fusion.2), kind=kCustom, calls=%fused_computation.clone.clone.clone.1 | custom fusion | bytes 8388736 | tf_op jit(solution)/shard_map/while/body/eval_jaxpr/gather | solution.py:53
  220.5 4.0 %maximum_convert_fusion.2 = bf16[4,8,256,256]{3,2,1,0:T(8,128)(2,1)S(1)} fusion(bf16[4,8,256,256]{3,2,1,0:T(8,128)(2,1)} %bitcast.126, bf16[32,1,256,256]{3,2,0,1:T(8,128)(2,1)} %get-tuple-element.689, s32[]{:T(128)S(6)} %select_n.224), kind=kOutput, calls=%fused_computation.8.clone.1 | convolution fusion | flops 1077936128 | bytes 8912900 | tf_op jit(solution)/shard_map/while/body/eval_jaxpr/scq,skcd->skqd/dot_general | solution.py:54
  224.5 7.3 %fusion.81 = f32[32,256,256]{1,2,0:T(8,128)S(1)} fusion(bf16[32,256,256]{1,2,0:T(8,128)(2,1)S(1)} %bitcast.124, f32[]{:T(128)} %get-tuple-element.704, f32[]{:T(128)} %get-tuple-element.701, f32[]{:T(128)} %get-tuple-element.699, f32[]{:T(128)} %get-tuple-element.697, f32[]{:T(128)} %get-tuple-element.695, f32[]{:T(128)} %get-tuple-element.694, ...), kind=kOutput, calls=%fused_computation.23.clone.1 | convolution fusion | flops 1075904512 | bytes 12589092 | tf_op jit(solution)/shard_map/while/body/eval_jaxpr/qa,nab->nqb/dot_general | solution.py:37
  231.8 8.6 %fusion.82 = f32[32,256]{1,0:T(8,128)S(1)} fusion(f32[32,256,256]{1,2,0:T(8,128)S(1)} %fusion.81, bf16[32,256,256]{1,2,0:T(8,128)(2,1)S(1)} %bitcast.125, f32[]{:T(128)} %get-tuple-element.713, f32[]{:T(128)} %get-tuple-element.712, f32[]{:T(128)} %get-tuple-element.711, f32[]{:T(128)} %get-tuple-element.710, f32[]{:T(128)} %get-tuple-element.709, ...), kind=kOutput, calls=%fused_computation.7.clone.1 | convolution fusion | flops 1080090624 | bytes 12621860 | tf_op jit(solution)/shard_map/while/body/eval_jaxpr/nqa,ba->nqb/dot_general | solution.py:38
  240.6 0.6 dynamic_slice.35
  243.0 5.0 %gather_fusion = bf16[32,256,256]{2,1,0:T(8,128)(2,1)} fusion(bf16[32,256,256]{2,1,0:T(8,128)(2,1)} %get-tuple-element.688, s32[1024]{0:T(1024)S(1)} %pad_clamp_fusion.2), kind=kCustom, calls=%fused_computation.clone.clone.clone.1 | custom fusion | bytes 8388736 | tf_op jit(solution)/shard_map/while/body/eval_jaxpr/gather | solution.py:53
  248.0 4.0 %maximum_convert_fusion.2 = bf16[4,8,256,256]{3,2,1,0:T(8,128)(2,1)S(1)} fusion(bf16[4,8,256,256]{3,2,1,0:T(8,128)(2,1)} %bitcast.126, bf16[32,1,256,256]{3,2,0,1:T(8,128)(2,1)} %get-tuple-element.689, s32[]{:T(128)S(6)} %select_n.224), kind=kOutput, calls=%fused_computation.8.clone.1 | convolution fusion | flops 1077936128 | bytes 8912900 | tf_op jit(solution)/shard_map/while/body/eval_jaxpr/scq,skcd->skqd/dot_general | solution.py:54
  252.0 7.3 %fusion.81 = f32[32,256,256]{1,2,0:T(8,128)S(1)} fusion(bf16[32,256,256]{1,2,0:T(8,128)(2,1)S(1)} %bitcast.124, f32[]{:T(128)} %get-tuple-element.704, f32[]{:T(128)} %get-tuple-element.701, f32[]{:T(128)} %get-tuple-element.699, f32[]{:T(128)} %get-tuple-element.697, f32[]{:T(128)} %get-tuple-element.695, f32[]{:T(128)} %get-tuple-element.694, ...), kind=kOutput, calls=%fused_computation.23.clone.1 | convolution fusion | flops 1075904512 | bytes 12589092 | tf_op jit(solution)/shard_map/while/body/eval_jaxpr/qa,nab->nqb/dot_general | solution.py:37
  259.4 8.6 %fusion.82 = f32[32,256]{1,0:T(8,128)S(1)} fusion(f32[32,256,256]{1,2,0:T(8,128)S(1)} %fusion.81, bf16[32,256,256]{1,2,0:T(8,128)(2,1)S(1)} %bitcast.125, f32[]{:T(128)} %get-tuple-element.713, f32[]{:T(128)} %get-tuple-element.712, f32[]{:T(128)} %get-tuple-element.711, f32[]{:T(128)} %get-tuple-element.710, f32[]{:T(128)} %get-tuple-element.709, ...), kind=kOutput, calls=%fused_computation.7.clone.1 | convolution fusion | flops 1080090624 | bytes 12621860 | tf_op jit(solution)/shard_map/while/body/eval_jaxpr/nqa,ba->nqb/dot_general | solution.py:38
  268.2 0.6 dynamic_slice.35
  270.6 5.0 %gather_fusion = bf16[32,256,256]{2,1,0:T(8,128)(2,1)} fusion(bf16[32,256,256]{2,1,0:T(8,128)(2,1)} %get-tuple-element.688, s32[1024]{0:T(1024)S(1)} %pad_clamp_fusion.2), kind=kCustom, calls=%fused_computation.clone.clone.clone.1 | custom fusion | bytes 8388736 | tf_op jit(solution)/shard_map/while/body/eval_jaxpr/gather | solution.py:53
  275.6 4.0 %maximum_convert_fusion.2 = bf16[4,8,256,256]{3,2,1,0:T(8,128)(2,1)S(1)} fusion(bf16[4,8,256,256]{3,2,1,0:T(8,128)(2,1)} %bitcast.126, bf16[32,1,256,256]{3,2,0,1:T(8,128)(2,1)} %get-tuple-element.689, s32[]{:T(128)S(6)} %select_n.224), kind=kOutput, calls=%fused_computation.8.clone.1 | convolution fusion | flops 1077936128 | bytes 8912900 | tf_op jit(solution)/shard_map/while/body/eval_jaxpr/scq,skcd->skqd/dot_general | solution.py:54
  279.6 7.3 %fusion.81 = f32[32,256,256]{1,2,0:T(8,128)S(1)} fusion(bf16[32,256,256]{1,2,0:T(8,128)(2,1)S(1)} %bitcast.124, f32[]{:T(128)} %get-tuple-element.704, f32[]{:T(128)} %get-tuple-element.701, f32[]{:T(128)} %get-tuple-element.699, f32[]{:T(128)} %get-tuple-element.697, f32[]{:T(128)} %get-tuple-element.695, f32[]{:T(128)} %get-tuple-element.694, ...), kind=kOutput, calls=%fused_computation.23.clone.1 | convolution fusion | flops 1075904512 | bytes 12589092 | tf_op jit(solution)/shard_map/while/body/eval_jaxpr/qa,nab->nqb/dot_general | solution.py:37
  286.9 8.6 %fusion.82 = f32[32,256]{1,0:T(8,128)S(1)} fusion(f32[32,256,256]{1,2,0:T(8,128)S(1)} %fusion.81, bf16[32,256,256]{1,2,0:T(8,128)(2,1)S(1)} %bitcast.125, f32[]{:T(128)} %get-tuple-element.713, f32[]{:T(128)} %get-tuple-element.712, f32[]{:T(128)} %get-tuple-element.711, f32[]{:T(128)} %get-tuple-element.710, f32[]{:T(128)} %get-tuple-element.709, ...), kind=kOutput, calls=%fused_computation.7.clone.1 | convolution fusion | flops 1080090624 | bytes 12621860 | tf_op jit(solution)/shard_map/while/body/eval_jaxpr/nqa,ba->nqb/dot_general | solution.py:38
  295.6 0.1 reduce_sum.48
  295.8 10.4 %all_to_all.17 = f32[32,1,8]{2,1,0:T(1,128)S(1)} all-to-all(f32[32,1,8]{2,1,0:T(1,128)S(1)} %bitcast.131), channel_id=1, replica_groups=mesh['db'=8,'pb'=4] {'db','pb'}, dimensions={0} | all-to-all | bytes 2048 | tf_op jit(solution)/shard_map/all_to_all | solution.py:100
  306.2 1.3 gather_fusion.1
  307.5 2.6 top_k.9
  (66 shorter events, 1.8 us)
Async XLA Ops:
  7.2 68.2 %all-gather.2.cloned.1.call-start = ((), (), s32[]{:S(2)}) async-start(), calls=%async_computation.2 | async-start | bytes 4325376 | tf_op jit(solution)/shard_map/all_gather | solution.py:92
  25.2 16.9 %all-to-all-start = ((s32[2,32,8]{2,0,1:T(2,128)}), s32[2,32,8]{2,0,1:T(2,128)S(1)}, u32[]{:S(2)}, u32[]{:S(2)}) async-start(s32[2,32,8]{2,0,1:T(2,128)} %copy.23), calls=%async_computation | async-start | bytes 65536 | tf_op jit(solution)/shard_map/all_to_all | solution.py:95
  32.5 6.5 %copy-start = (bf16[32,256,256]{2,1,0:T(8,128)(2,1)S(1)}, bf16[32,256,256]{2,1,0:T(8,128)(2,1)}, u32[]{:S(2)}) copy-start(bf16[32,256,256]{2,1,0:T(8,128)(2,1)} %param.8) | copy-start | bytes 12582916
  307.5 2.7 copy-start.1
Sparse Core Ops, SparseCore 0:
  11.0 64.3 all-gather.1
where the time goes:
time: 319 us; the launch traced here: 317 us
  matrix products  160 us (50%)
  local copies, waits for them, and re-layouts  63.6 us (20%)
  waiting for transfers between devices  33.2 us (10%)
  other arithmetic  14.3 us (4%)
  between operations  14.2 us (4%)
  loops' own time  14 us (4%)
  blocking collectives  10.4 us (3%)
  starting transfers between devices  7.36 us (2%)
    dot_general x8, matrix products, finish_pairs(): jnp.einsum('nqa,ba->nqb', rectified, conv_db, preferred_element_type=jnp....  69.1 us
    dot_general x8, matrix products, finish_pairs(): jnp.einsum('qa,nab->nqb', conv_query, rectified, preferred_element_type=j...  58.8 us
    gather x8, local copies, waits for them, and re-layouts, score_block(): images = db_unit[slot_block]  39.8 us
    all_gather x1, waiting for transfers between devices, body(): gathered = lax.all_gather(query_unit, ('db', 'pb'), axis=0, tiled=True)  33.2 us
    dot_general x8, matrix products, score_block(): jnp.einsum('scq,skcd->skqd', group_block[:, 0], images, preferred_element...  32.1 us
    another operation x1, loops' own time, shard_scores(): return lax.map(score_block, starts).reshape(source_count, width)  14 us
    all_to_all x1, blocking collectives, body(): lax.all_to_all(found, ('db', 'pb'), split_axis=0, concat_axis=0, tiled=True)  10.4 us
    all_to_all x1, starting transfers between devices, body(): lax.all_to_all(requests, ('db', 'pb'), split_axis=1, concat_axis=1, tiled...  7.33 us
  transfers between devices with their start and end apart: 2, of which 1 were waited for; matrix products, arithmetic and copies ran while one was open for 8% of the time, Pallas kernels for 0%

commit v1 on v0

--- a/solution.py
+++ b/solution.py
@@ -8,6 +8,28 @@
 TOPK = 100
 epsilon = 1e-06
 score_scale = 8.0
+
+
+def joined_along(blocks, dim):
+    blocks = jnp.moveaxis(blocks, 0, dim)
+    lengths = blocks.shape
+    return blocks.reshape(*lengths[:dim], lengths[dim] * lengths[dim + 1], *lengths[dim + 2 :])
+
+
+def doubled(shard, axis):
+    devices = lax.axis_size(axis)
+    blocks = shard[None]
+    for level in range(devices.bit_length() - 1):
+        bit = 1 << level
+        other = lax.ppermute(blocks, axis, [(i, i ^ bit) for i in range(devices)])
+        both = jnp.stack([blocks, other])
+        upper = lax.axis_index(axis) >> level & 1
+        blocks = jnp.where(upper == 0, both, both[::-1]).reshape(-1, *shard.shape)
+    return blocks
+
+
+def collect(x, axis, dim):
+    return joined_along(doubled(x, axis), dim)
 
 
 def unit_maps(maps):
@@ -89,7 +111,7 @@
     send_slot = empty.at[shard_of, bucket_pos].set(slot_of)
     send_query = empty.at[shard_of, bucket_pos].set(query_of)
     requests = jnp.stack([send_slot, send_query])
-    gathered = lax.all_gather(query_unit, ("db", "pb"), axis=0, tiled=True)
+    gathered = collect(query_unit, ("db", "pb"), 0)
     found = shard_scores(
         gathered,
         lax.all_to_all(requests, ("db", "pb"), split_axis=1, concat_axis=1, tiled=True)[0],

time: 319 us -> 343 us (1.075)
  waiting for transfers between devices: 33.2 us -> 59.7 us
  between operations: 14.2 us -> 0.9 us
  starting transfers between devices: 7.36 us -> 13.9 us
  other arithmetic: 14.3 us -> 18.5 us
    ppermute x0 -> x5, waiting for transfers between devices: none -> 40 us  [doubled(): other = lax.ppermute(blocks, axis, [(i, i ^ bit) for i in range(devices)])]
    all_gather x1 -> x0, waiting for transfers between devices: 33.2 us -> none  [body(): gathered = lax.all_gather(query_unit, ('db', 'pb'), axis=0, tiled=True)]
    all_to_all x1, waiting for transfers between devices: 0.01 us -> 19.7 us  [body(): lax.all_to_all(requests, ('db', 'pb'), split_axis=1, concat_axis=1, tiled...]
    ppermute x0 -> x5, starting transfers between devices: none -> 8.92 us  [doubled(): other = lax.ppermute(blocks, axis, [(i, i ^ bit) for i in range(devices)])]
    select_n x0 -> x4, other arithmetic: none -> 3.86 us  [doubled(): blocks = jnp.where(upper == 0, both, both[::-1]).reshape(-1, *shard.shape)]
  transfers between devices with their start and end apart: 2 -> 6, of which waited for: 1 -> 5; matrix products, arithmetic and copies ran while one was open for 8% -> 6% of each run, Pallas kernels for 0% -> 0%
where the time goes in v1:
time: 343 us; the launch traced here: 341 us
  matrix products  160 us (47%)
  local copies, waits for them, and re-layouts  61.6 us (18%)
  waiting for transfers between devices  59.7 us (17%)
  other arithmetic  18.5 us (5%)
  loops' own time  14 us (4%)
  starting transfers between devices  13.9 us (4%)
  blocking collectives  12.7 us (4%)
    dot_general x8, matrix products, finish_pairs(): jnp.einsum('nqa,ba->nqb', rectified, conv_db, preferred_element_type=jnp....  69 us
    dot_general x8, matrix products, finish_pairs(): jnp.einsum('qa,nab->nqb', conv_query, rectified, preferred_element_type=j...  58.7 us
    ppermute x5, waiting for transfers between devices, doubled(): other = lax.ppermute(blocks, axis, [(i, i ^ bit) for i in range(devices)])  40 us
    gather x8, local copies, waits for them, and re-layouts, score_block(): images = db_unit[slot_block]  39.8 us
    dot_general x8, matrix products, score_block(): jnp.einsum('scq,skcd->skqd', group_block[:, 0], images, preferred_element...  32.1 us
    all_to_all x1, waiting for transfers between devices, body(): lax.all_to_all(requests, ('db', 'pb'), split_axis=1, concat_axis=1, tiled...  19.7 us
    another operation x1, loops' own time, shard_scores(): return lax.map(score_block, starts).reshape(source_count, width)  14 us
    all_to_all x1, blocking collectives, body(): lax.all_to_all(found, ('db', 'pb'), split_axis=0, concat_axis=0, tiled=True)  12.7 us
  transfers between devices with their start and end apart: 6, of which 5 were waited for; matrix products, arithmetic and copies ran while one was open for 6% of the time, Pallas kernels for 0%

profile of v1, /device:TPU:0, one launch (start us, length us, event | category | flops | bytes accessed | tf_op | source)
XLA Modules:
  0.0 341.0 jit_solution(12392830739413966655)
XLA Ops:
  0.6 1.0 fusion.53
  1.6 0.9 fusion.58
  2.5 3.1 collective-permute-start
  5.7 3.5 %collective-permute-done = bf16[1,1,256,256]{3,2,1,0:T(8,128)(2,1)S(1)} collective-permute-done((bf16[1,1,256,256]{3,2,1,0:T(8,128)(2,1)S(1)}, bf16[1,1,256,256]{3,2,1,0:T(8,128)(2,1)S(1)}, u32[]{:S(2)}, u32[]{:S(2)}) %collective-permute-start) | collective-permute-done | bytes 131104 | tf_op jit(solution)/shard_map/ppermute | solution.py:24
  9.3 2.8 collective-permute-start.1
  12.1 11.2 %collective-permute-done.1 = bf16[2,1,256,256]{3,2,0,1:T(8,128)(2,1)S(1)} collective-permute-done((bf16[2,1,256,256]{3,2,0,1:T(8,128)(2,1)S(1)}, bf16[2,1,256,256]{3,2,0,1:T(8,128)(2,1)S(1)}, u32[]{:S(2)}, u32[]{:S(2)}) %collective-permute-start.1) | collective-permute-done | bytes 262176 | tf_op jit(solution)/shard_map/ppermute | solution.py:24
  23.6 1.9 collective-permute-done.2
  25.7 1.4 collective-permute-start.3
  27.7 23.3 %collective-permute-done.3 = bf16[8,1,256,256]{3,2,0,1:T(8,128)(2,1)S(1)} collective-permute-done((bf16[8,1,256,256]{3,2,0,1:T(8,128)(2,1)S(1)}, bf16[8,1,256,256]{3,2,0,1:T(8,128)(2,1)S(1)}, u32[]{:S(2)}, u32[]{:S(2)}) %collective-permute-start.3) | collective-permute-done | bytes 1048608 | tf_op jit(solution)/shard_map/ppermute | solution.py:24
  51.7 1.5 collective-permute-start.4
  53.2 6.4 %scatter_fusion = s32[32,8]{0,1:T(8,128)S(1)} fusion(s32[32,8]{0,1:T(8,128)S(1)} %broadcast_in_dim.13.clone.1, s32[128]{0:T(128)S(1)} %fusion.64, s32[128]{0:T(128)S(1)} %get-tuple-element.431), kind=kCustom, calls=%fused_computation.2 | custom fusion | bytes 2560 | tf_op jit(solution)/shard_map/scatter | solution.py:111
  59.7 6.4 %scatter_fusion.1 = s32[32,8]{0,1:T(8,128)S(1)} fusion(s32[32,8]{0,1:T(8,128)S(1)} %broadcast_in_dim.13.clone, s32[128]{0:T(128)S(1)} %fusion.64, s32[128]{0:T(128)S(1)} %and_select_fusion.2), kind=kCustom, calls=%fused_computation.3 | custom fusion | bytes 2560 | tf_op jit(solution)/shard_map/scatter | solution.py:112
  66.1 0.7 copy.26
  66.8 5.0 %all-to-all-start = ((s32[2,32,8]{2,0,1:T(2,128)}), s32[2,32,8]{2,0,1:T(2,128)S(1)}, u32[]{:S(2)}, u32[]{:S(2)}) async-start(s32[2,32,8]{2,0,1:T(2,128)} %copy.26), calls=%async_computation | async-start | bytes 65536 | tf_op jit(solution)/shard_map/all_to_all | solution.py:117
  71.8 0.7 fusion.67
  72.5 0.7 fusion.66
  73.2 3.1 fusion.51
  76.3 3.0 fusion.52
  79.3 19.7 %all-to-all-done = s32[2,32,8]{2,0,1:T(2,128)S(1)} async-done(((s32[2,32,8]{2,0,1:T(2,128)}), s32[2,32,8]{2,0,1:T(2,128)S(1)}, u32[]{:S(2)}, u32[]{:S(2)}) %all-to-all-start) | async-done | bytes 2080 | tf_op jit(solution)/shard_map/all_to_all | solution.py:117
  99.1 2.0 pad_maximum_fusion
  101.0 3.1 reverse_select_fusion
  104.1 220.1 %while.14 = (s32[]{:T(128)}, f32[8,32]{1,0:T(8,128)S(1)}, s32[8]{0:T(128)S(1)}, s32[32,8]{1,0:T(8,128)S(1)}, bf16[32,256,256]{2,1,0:T(8,128)(2,1)}, /*index=5*/b...) while((s32[]{:T(128)}, f32[8,32]{1,0:T(8,128)S(1)}, ...), condition=%wide.region_9.10_spmd.clone.clone, body=%wide.region_6.9_spmd.clone.clone.sunk | while | flops 3233940480 | bytes 42551080 | solution.py:85
  106.5 5.0 %gather_fusion = bf16[32,256,256]{2,1,0:T(8,128)(2,1)} fusion(bf16[32,256,256]{2,1,0:T(8,128)(2,1)} %get-tuple-element.692, s32[1024]{0:T(1024)S(1)} %pad_clamp_fusion.2), kind=kCustom, calls=%fused_computation.clone.clone.clone.1 | custom fusion | bytes 8388736 | tf_op jit(solution)/shard_map/while/body/eval_jaxpr/gather | solution.py:75
  111.5 4.0 %maximum_convert_fusion.2 = bf16[4,8,256,256]{3,2,1,0:T(8,128)(2,1)S(1)} fusion(bf16[4,8,256,256]{3,2,1,0:T(8,128)(2,1)} %bitcast.147, bf16[32,1,256,256]{3,2,0,1:T(8,128)(2,1)} %get-tuple-element.693, s32[]{:T(128)S(6)} %select_n.292), kind=kOutput, calls=%fused_computation.8.clone.1 | convolution fusion | flops 1077936128 | bytes 8912900 | tf_op jit(solution)/shard_map/while/body/eval_jaxpr/scq,skcd->skqd/dot_general | solution.py:76
  115.5 7.3 %fusion.85 = f32[32,256,256]{1,2,0:T(8,128)S(1)} fusion(bf16[32,256,256]{1,2,0:T(8,128)(2,1)S(1)} %bitcast.145, f32[]{:T(128)} %get-tuple-element.708, f32[]{:T(128)} %get-tuple-element.705, f32[]{:T(128)} %get-tuple-element.703, f32[]{:T(128)} %get-tuple-element.701, f32[]{:T(128)} %get-tuple-element.699, f32[]{:T(128)} %get-tuple-element.698, ...), kind=kOutput, calls=%fused_computation.23.clone.1 | convolution fusion | flops 1075904512 | bytes 12589092 | tf_op jit(solution)/shard_map/while/body/eval_jaxpr/qa,nab->nqb/dot_general | solution.py:59
  122.9 8.6 %fusion.86 = f32[32,256]{1,0:T(8,128)S(1)} fusion(f32[32,256,256]{1,2,0:T(8,128)S(1)} %fusion.85, bf16[32,256,256]{1,2,0:T(8,128)(2,1)S(1)} %bitcast.146, f32[]{:T(128)} %get-tuple-element.717, f32[]{:T(128)} %get-tuple-element.716, f32[]{:T(128)} %get-tuple-element.715, f32[]{:T(128)} %get-tuple-element.714, f32[]{:T(128)} %get-tuple-element.713, ...), kind=kOutput, calls=%fused_computation.7.clone.1 | convolution fusion | flops 1080090624 | bytes 12621860 | tf_op jit(solution)/shard_map/while/body/eval_jaxpr/nqa,ba->nqb/dot_general | solution.py:60
  131.7 0.6 dynamic_slice.35
  134.0 5.0 %gather_fusion = bf16[32,256,256]{2,1,0:T(8,128)(2,1)} fusion(bf16[32,256,256]{2,1,0:T(8,128)(2,1)} %get-tuple-element.692, s32[1024]{0:T(1024)S(1)} %pad_clamp_fusion.2), kind=kCustom, calls=%fused_computation.clone.clone.clone.1 | custom fusion | bytes 8388736 | tf_op jit(solution)/shard_map/while/body/eval_jaxpr/gather | solution.py:75
  139.0 4.0 %maximum_convert_fusion.2 = bf16[4,8,256,256]{3,2,1,0:T(8,128)(2,1)S(1)} fusion(bf16[4,8,256,256]{3,2,1,0:T(8,128)(2,1)} %bitcast.147, bf16[32,1,256,256]{3,2,0,1:T(8,128)(2,1)} %get-tuple-element.693, s32[]{:T(128)S(6)} %select_n.292), kind=kOutput, calls=%fused_computation.8.clone.1 | convolution fusion | flops 1077936128 | bytes 8912900 | tf_op jit(solution)/shard_map/while/body/eval_jaxpr/scq,skcd->skqd/dot_general | solution.py:76
  143.0 7.3 %fusion.85 = f32[32,256,256]{1,2,0:T(8,128)S(1)} fusion(bf16[32,256,256]{1,2,0:T(8,128)(2,1)S(1)} %bitcast.145, f32[]{:T(128)} %get-tuple-element.708, f32[]{:T(128)} %get-tuple-element.705, f32[]{:T(128)} %get-tuple-element.703, f32[]{:T(128)} %get-tuple-element.701, f32[]{:T(128)} %get-tuple-element.699, f32[]{:T(128)} %get-tuple-element.698, ...), kind=kOutput, calls=%fused_computation.23.clone.1 | convolution fusion | flops 1075904512 | bytes 12589092 | tf_op jit(solution)/shard_map/while/body/eval_jaxpr/qa,nab->nqb/dot_general | solution.py:59
  150.4 8.6 %fusion.86 = f32[32,256]{1,0:T(8,128)S(1)} fusion(f32[32,256,256]{1,2,0:T(8,128)S(1)} %fusion.85, bf16[32,256,256]{1,2,0:T(8,128)(2,1)S(1)} %bitcast.146, f32[]{:T(128)} %get-tuple-element.717, f32[]{:T(128)} %get-tuple-element.716, f32[]{:T(128)} %get-tuple-element.715, f32[]{:T(128)} %get-tuple-element.714, f32[]{:T(128)} %get-tuple-element.713, ...), kind=kOutput, calls=%fused_computation.7.clone.1 | convolution fusion | flops 1080090624 | bytes 12621860 | tf_op jit(solution)/shard_map/while/body/eval_jaxpr/nqa,ba->nqb/dot_general | solution.py:60
  159.2 0.6 dynamic_slice.35
  161.6 5.0 %gather_fusion = bf16[32,256,256]{2,1,0:T(8,128)(2,1)} fusion(bf16[32,256,256]{2,1,0:T(8,128)(2,1)} %get-tuple-element.692, s32[1024]{0:T(1024)S(1)} %pad_clamp_fusion.2), kind=kCustom, calls=%fused_computation.clone.clone.clone.1 | custom fusion | bytes 8388736 | tf_op jit(solution)/shard_map/while/body/eval_jaxpr/gather | solution.py:75
  166.5 4.0 %maximum_convert_fusion.2 = bf16[4,8,256,256]{3,2,1,0:T(8,128)(2,1)S(1)} fusion(bf16[4,8,256,256]{3,2,1,0:T(8,128)(2,1)} %bitcast.147, bf16[32,1,256,256]{3,2,0,1:T(8,128)(2,1)} %get-tuple-element.693, s32[]{:T(128)S(6)} %select_n.292), kind=kOutput, calls=%fused_computation.8.clone.1 | convolution fusion | flops 1077936128 | bytes 8912900 | tf_op jit(solution)/shard_map/while/body/eval_jaxpr/scq,skcd->skqd/dot_general | solution.py:76
  170.6 7.3 %fusion.85 = f32[32,256,256]{1,2,0:T(8,128)S(1)} fusion(bf16[32,256,256]{1,2,0:T(8,128)(2,1)S(1)} %bitcast.145, f32[]{:T(128)} %get-tuple-element.708, f32[]{:T(128)} %get-tuple-element.705, f32[]{:T(128)} %get-tuple-element.703, f32[]{:T(128)} %get-tuple-element.701, f32[]{:T(128)} %get-tuple-element.699, f32[]{:T(128)} %get-tuple-element.698, ...), kind=kOutput, calls=%fused_computation.23.clone.1 | convolution fusion | flops 1075904512 | bytes 12589092 | tf_op jit(solution)/shard_map/while/body/eval_jaxpr/qa,nab->nqb/dot_general | solution.py:59
  177.9 8.6 %fusion.86 = f32[32,256]{1,0:T(8,128)S(1)} fusion(f32[32,256,256]{1,2,0:T(8,128)S(1)} %fusion.85, bf16[32,256,256]{1,2,0:T(8,128)(2,1)S(1)} %bitcast.146, f32[]{:T(128)} %get-tuple-element.717, f32[]{:T(128)} %get-tuple-element.716, f32[]{:T(128)} %get-tuple-element.715, f32[]{:T(128)} %get-tuple-element.714, f32[]{:T(128)} %get-tuple-element.713, ...), kind=kOutput, calls=%fused_computation.7.clone.1 | convolution fusion | flops 1080090624 | bytes 12621860 | tf_op jit(solution)/shard_map/while/body/eval_jaxpr/nqa,ba->nqb/dot_general | solution.py:60
  186.7 0.6 dynamic_slice.35
  189.1 5.0 %gather_fusion = bf16[32,256,256]{2,1,0:T(8,128)(2,1)} fusion(bf16[32,256,256]{2,1,0:T(8,128)(2,1)} %get-tuple-element.692, s32[1024]{0:T(1024)S(1)} %pad_clamp_fusion.2), kind=kCustom, calls=%fused_computation.clone.clone.clone.1 | custom fusion | bytes 8388736 | tf_op jit(solution)/shard_map/while/body/eval_jaxpr/gather | solution.py:75
  194.1 4.0 %maximum_convert_fusion.2 = bf16[4,8,256,256]{3,2,1,0:T(8,128)(2,1)S(1)} fusion(bf16[4,8,256,256]{3,2,1,0:T(8,128)(2,1)} %bitcast.147, bf16[32,1,256,256]{3,2,0,1:T(8,128)(2,1)} %get-tuple-element.693, s32[]{:T(128)S(6)} %select_n.292), kind=kOutput, calls=%fused_computation.8.clone.1 | convolution fusion | flops 1077936128 | bytes 8912900 | tf_op jit(solution)/shard_map/while/body/eval_jaxpr/scq,skcd->skqd/dot_general | solution.py:76
  198.1 7.3 %fusion.85 = f32[32,256,256]{1,2,0:T(8,128)S(1)} fusion(bf16[32,256,256]{1,2,0:T(8,128)(2,1)S(1)} %bitcast.145, f32[]{:T(128)} %get-tuple-element.708, f32[]{:T(128)} %get-tuple-element.705, f32[]{:T(128)} %get-tuple-element.703, f32[]{:T(128)} %get-tuple-element.701, f32[]{:T(128)} %get-tuple-element.699, f32[]{:T(128)} %get-tuple-element.698, ...), kind=kOutput, calls=%fused_computation.23.clone.1 | convolution fusion | flops 1075904512 | bytes 12589092 | tf_op jit(solution)/shard_map/while/body/eval_jaxpr/qa,nab->nqb/dot_general | solution.py:59
  205.4 8.6 %fusion.86 = f32[32,256]{1,0:T(8,128)S(1)} fusion(f32[32,256,256]{1,2,0:T(8,128)S(1)} %fusion.85, bf16[32,256,256]{1,2,0:T(8,128)(2,1)S(1)} %bitcast.146, f32[]{:T(128)} %get-tuple-element.717, f32[]{:T(128)} %get-tuple-element.716, f32[]{:T(128)} %get-tuple-element.715, f32[]{:T(128)} %get-tuple-element.714, f32[]{:T(128)} %get-tuple-element.713, ...), kind=kOutput, calls=%fused_computation.7.clone.1 | convolution fusion | flops 1080090624 | bytes 12621860 | tf_op jit(solution)/shard_map/while/body/eval_jaxpr/nqa,ba->nqb/dot_general | solution.py:60
  214.2 0.6 dynamic_slice.35
  216.6 5.0 %gather_fusion = bf16[32,256,256]{2,1,0:T(8,128)(2,1)} fusion(bf16[32,256,256]{2,1,0:T(8,128)(2,1)} %get-tuple-element.692, s32[1024]{0:T(1024)S(1)} %pad_clamp_fusion.2), kind=kCustom, calls=%fused_computation.clone.clone.clone.1 | custom fusion | bytes 8388736 | tf_op jit(solution)/shard_map/while/body/eval_jaxpr/gather | solution.py:75
  221.6 4.0 %maximum_convert_fusion.2 = bf16[4,8,256,256]{3,2,1,0:T(8,128)(2,1)S(1)} fusion(bf16[4,8,256,256]{3,2,1,0:T(8,128)(2,1)} %bitcast.147, bf16[32,1,256,256]{3,2,0,1:T(8,128)(2,1)} %get-tuple-element.693, s32[]{:T(128)S(6)} %select_n.292), kind=kOutput, calls=%fused_computation.8.clone.1 | convolution fusion | flops 1077936128 | bytes 8912900 | tf_op jit(solution)/shard_map/while/body/eval_jaxpr/scq,skcd->skqd/dot_general | solution.py:76
  225.6 7.3 %fusion.85 = f32[32,256,256]{1,2,0:T(8,128)S(1)} fusion(bf16[32,256,256]{1,2,0:T(8,128)(2,1)S(1)} %bitcast.145, f32[]{:T(128)} %get-tuple-element.708, f32[]{:T(128)} %get-tuple-element.705, f32[]{:T(128)} %get-tuple-element.703, f32[]{:T(128)} %get-tuple-element.701, f32[]{:T(128)} %get-tuple-element.699, f32[]{:T(128)} %get-tuple-element.698, ...), kind=kOutput, calls=%fused_computation.23.clone.1 | convolution fusion | flops 1075904512 | bytes 12589092 | tf_op jit(solution)/shard_map/while/body/eval_jaxpr/qa,nab->nqb/dot_general | solution.py:59
  232.9 8.6 %fusion.86 = f32[32,256]{1,0:T(8,128)S(1)} fusion(f32[32,256,256]{1,2,0:T(8,128)S(1)} %fusion.85, bf16[32,256,256]{1,2,0:T(8,128)(2,1)S(1)} %bitcast.146, f32[]{:T(128)} %get-tuple-element.717, f32[]{:T(128)} %get-tuple-element.716, f32[]{:T(128)} %get-tuple-element.715, f32[]{:T(128)} %get-tuple-element.714, f32[]{:T(128)} %get-tuple-element.713, ...), kind=kOutput, calls=%fused_computation.7.clone.1 | convolution fusion | flops 1080090624 | bytes 12621860 | tf_op jit(solution)/shard_map/while/body/eval_jaxpr/nqa,ba->nqb/dot_general | solution.py:60
  241.7 0.6 dynamic_slice.35
  244.1 5.0 %gather_fusion = bf16[32,256,256]{2,1,0:T(8,128)(2,1)} fusion(bf16[32,256,256]{2,1,0:T(8,128)(2,1)} %get-tuple-element.692, s32[1024]{0:T(1024)S(1)} %pad_clamp_fusion.2), kind=kCustom, calls=%fused_computation.clone.clone.clone.1 | custom fusion | bytes 8388736 | tf_op jit(solution)/shard_map/while/body/eval_jaxpr/gather | solution.py:75
  249.1 4.0 %maximum_convert_fusion.2 = bf16[4,8,256,256]{3,2,1,0:T(8,128)(2,1)S(1)} fusion(bf16[4,8,256,256]{3,2,1,0:T(8,128)(2,1)} %bitcast.147, bf16[32,1,256,256]{3,2,0,1:T(8,128)(2,1)} %get-tuple-element.693, s32[]{:T(128)S(6)} %select_n.292), kind=kOutput, calls=%fused_computation.8.clone.1 | convolution fusion | flops 1077936128 | bytes 8912900 | tf_op jit(solution)/shard_map/while/body/eval_jaxpr/scq,skcd->skqd/dot_general | solution.py:76
  253.1 7.3 %fusion.85 = f32[32,256,256]{1,2,0:T(8,128)S(1)} fusion(bf16[32,256,256]{1,2,0:T(8,128)(2,1)S(1)} %bitcast.145, f32[]{:T(128)} %get-tuple-element.708, f32[]{:T(128)} %get-tuple-element.705, f32[]{:T(128)} %get-tuple-element.703, f32[]{:T(128)} %get-tuple-element.701, f32[]{:T(128)} %get-tuple-element.699, f32[]{:T(128)} %get-tuple-element.698, ...), kind=kOutput, calls=%fused_computation.23.clone.1 | convolution fusion | flops 1075904512 | bytes 12589092 | tf_op jit(solution)/shard_map/while/body/eval_jaxpr/qa,nab->nqb/dot_general | solution.py:59
  260.5 8.6 %fusion.86 = f32[32,256]{1,0:T(8,128)S(1)} fusion(f32[32,256,256]{1,2,0:T(8,128)S(1)} %fusion.85, bf16[32,256,256]{1,2,0:T(8,128)(2,1)S(1)} %bitcast.146, f32[]{:T(128)} %get-tuple-element.717, f32[]{:T(128)} %get-tuple-element.716, f32[]{:T(128)} %get-tuple-element.715, f32[]{:T(128)} %get-tuple-element.714, f32[]{:T(128)} %get-tuple-element.713, ...), kind=kOutput, calls=%fused_computation.7.clone.1 | convolution fusion | flops 1080090624 | bytes 12621860 | tf_op jit(solution)/shard_map/while/body/eval_jaxpr/nqa,ba->nqb/dot_general | solution.py:60
  269.3 0.6 dynamic_slice.35
  271.6 5.0 %gather_fusion = bf16[32,256,256]{2,1,0:T(8,128)(2,1)} fusion(bf16[32,256,256]{2,1,0:T(8,128)(2,1)} %get-tuple-element.692, s32[1024]{0:T(1024)S(1)} %pad_clamp_fusion.2), kind=kCustom, calls=%fused_computation.clone.clone.clone.1 | custom fusion | bytes 8388736 | tf_op jit(solution)/shard_map/while/body/eval_jaxpr/gather | solution.py:75
  276.6 4.0 %maximum_convert_fusion.2 = bf16[4,8,256,256]{3,2,1,0:T(8,128)(2,1)S(1)} fusion(bf16[4,8,256,256]{3,2,1,0:T(8,128)(2,1)} %bitcast.147, bf16[32,1,256,256]{3,2,0,1:T(8,128)(2,1)} %get-tuple-element.693, s32[]{:T(128)S(6)} %select_n.292), kind=kOutput, calls=%fused_computation.8.clone.1 | convolution fusion | flops 1077936128 | bytes 8912900 | tf_op jit(solution)/shard_map/while/body/eval_jaxpr/scq,skcd->skqd/dot_general | solution.py:76
  280.6 7.3 %fusion.85 = f32[32,256,256]{1,2,0:T(8,128)S(1)} fusion(bf16[32,256,256]{1,2,0:T(8,128)(2,1)S(1)} %bitcast.145, f32[]{:T(128)} %get-tuple-element.708, f32[]{:T(128)} %get-tuple-element.705, f32[]{:T(128)} %get-tuple-element.703, f32[]{:T(128)} %get-tuple-element.701, f32[]{:T(128)} %get-tuple-element.699, f32[]{:T(128)} %get-tuple-element.698, ...), kind=kOutput, calls=%fused_computation.23.clone.1 | convolution fusion | flops 1075904512 | bytes 12589092 | tf_op jit(solution)/shard_map/while/body/eval_jaxpr/qa,nab->nqb/dot_general | solution.py:59
  288.0 8.6 %fusion.86 = f32[32,256]{1,0:T(8,128)S(1)} fusion(f32[32,256,256]{1,2,0:T(8,128)S(1)} %fusion.85, bf16[32,256,256]{1,2,0:T(8,128)(2,1)S(1)} %bitcast.146, f32[]{:T(128)} %get-tuple-element.717, f32[]{:T(128)} %get-tuple-element.716, f32[]{:T(128)} %get-tuple-element.715, f32[]{:T(128)} %get-tuple-element.714, f32[]{:T(128)} %get-tuple-element.713, ...), kind=kOutput, calls=%fused_computation.7.clone.1 | convolution fusion | flops 1080090624 | bytes 12621860 | tf_op jit(solution)/shard_map/while/body/eval_jaxpr/nqa,ba->nqb/dot_general | solution.py:60
  296.8 0.6 dynamic_slice.35
  299.2 5.0 %gather_fusion = bf16[32,256,256]{2,1,0:T(8,128)(2,1)} fusion(bf16[32,256,256]{2,1,0:T(8,128)(2,1)} %get-tuple-element.692, s32[1024]{0:T(1024)S(1)} %pad_clamp_fusion.2), kind=kCustom, calls=%fused_computation.clone.clone.clone.1 | custom fusion | bytes 8388736 | tf_op jit(solution)/shard_map/while/body/eval_jaxpr/gather | solution.py:75
  304.1 4.0 %maximum_convert_fusion.2 = bf16[4,8,256,256]{3,2,1,0:T(8,128)(2,1)S(1)} fusion(bf16[4,8,256,256]{3,2,1,0:T(8,128)(2,1)} %bitcast.147, bf16[32,1,256,256]{3,2,0,1:T(8,128)(2,1)} %get-tuple-element.693, s32[]{:T(128)S(6)} %select_n.292), kind=kOutput, calls=%fused_computation.8.clone.1 | convolution fusion | flops 1077936128 | bytes 8912900 | tf_op jit(solution)/shard_map/while/body/eval_jaxpr/scq,skcd->skqd/dot_general | solution.py:76
  308.2 7.3 %fusion.85 = f32[32,256,256]{1,2,0:T(8,128)S(1)} fusion(bf16[32,256,256]{1,2,0:T(8,128)(2,1)S(1)} %bitcast.145, f32[]{:T(128)} %get-tuple-element.708, f32[]{:T(128)} %get-tuple-element.705, f32[]{:T(128)} %get-tuple-element.703, f32[]{:T(128)} %get-tuple-element.701, f32[]{:T(128)} %get-tuple-element.699, f32[]{:T(128)} %get-tuple-element.698, ...), kind=kOutput, calls=%fused_computation.23.clone.1 | convolution fusion | flops 1075904512 | bytes 12589092 | tf_op jit(solution)/shard_map/while/body/eval_jaxpr/qa,nab->nqb/dot_general | solution.py:59
  315.5 8.6 %fusion.86 = f32[32,256]{1,0:T(8,128)S(1)} fusion(f32[32,256,256]{1,2,0:T(8,128)S(1)} %fusion.85, bf16[32,256,256]{1,2,0:T(8,128)(2,1)S(1)} %bitcast.146, f32[]{:T(128)} %get-tuple-element.717, f32[]{:T(128)} %get-tuple-element.716, f32[]{:T(128)} %get-tuple-element.715, f32[]{:T(128)} %get-tuple-element.714, f32[]{:T(128)} %get-tuple-element.713, ...), kind=kOutput, calls=%fused_computation.7.clone.1 | convolution fusion | flops 1080090624 | bytes 12621860 | tf_op jit(solution)/shard_map/while/body/eval_jaxpr/nqa,ba->nqb/dot_general | solution.py:60
  324.4 12.7 %all_to_all.17 = f32[32,1,8]{2,1,0:T(1,128)S(1)} all-to-all(f32[32,1,8]{2,1,0:T(1,128)S(1)} %bitcast.162), channel_id=1, replica_groups=mesh['db'=8,'pb'=4] {'db','pb'}, dimensions={0} | all-to-all | bytes 2048 | tf_op jit(solution)/shard_map/all_to_all | solution.py:122
  337.0 1.3 gather_fusion.1
  338.3 2.6 top_k.9
  (89 shorter events, 4.5 us)
Async XLA Ops:
  0.6 26.6 %copy-start.3 = (s32[1,128]{1,0:T(1,128)S(1)}, s32[1,128]{1,0:T(1,128)}, u32[]{:S(2)}) copy-start(s32[1,128]{1,0:T(1,128)} %param.9) | copy-start | bytes 1540
  2.5 6.6 %collective-permute-start = (bf16[1,1,256,256]{3,2,1,0:T(8,128)(2,1)S(1)}, bf16[1,1,256,256]{3,2,1,0:T(8,128)(2,1)S(1)}, u32[]{:S(2)}, u32[]{:S(2)}) collective-permute-start(bf16[1,1,256,256]{3,2,1,0:T(8,128)(2,1)S(1)} %get-tuple-element.412), channel_id=1, source_target_pairs={{0,1},{1,0},{2,3},{3,2},{4,5},{5,4},{6,7},{7,6},{8,9},{9,8},{10,11... | collective-permute-start | bytes 393224 | tf_op jit(solution)/shard_map/ppermute | solution.py:24
  9.3 14.1 %collective-permute-start.1 = (bf16[2,1,256,256]{3,2,0,1:T(8,128)(2,1)S(1)}, bf16[2,1,256,256]{3,2,0,1:T(8,128)(2,1)S(1)}, u32[]{:S(2)}, u32[]{:S(2)}) collective-permute-start(bf16[2,1,256,256]{3,2,0,1:T(8,128)(2,1)S(1)} %get-tuple-element.410), channel_id=1, source_target_pairs={{0,2},{1,3},{2,0},{3,1},{4,6},{5,7},{6,4},{7,5},{8,10},{9,11},{10,... | collective-permute-start | bytes 786440 | tf_op jit(solution)/shard_map/ppermute | solution.py:24
  23.5 2.0 collective-permute-start.2
  25.7 25.3 %collective-permute-start.3 = (bf16[8,1,256,256]{3,2,0,1:T(8,128)(2,1)S(1)}, bf16[8,1,256,256]{3,2,0,1:T(8,128)(2,1)S(1)}, u32[]{:S(2)}, u32[]{:S(2)}) collective-permute-start(bf16[8,1,256,256]{3,2,0,1:T(8,128)(2,1)S(1)} %bitcast.154), channel_id=1, source_target_pairs={{0,8},{1,9},{2,10},{3,11},{4,12},{5,13},{6,14},{7,15},{8,0},{9,1},... | collective-permute-start | bytes 3145736 | tf_op jit(solution)/shard_map/ppermute | solution.py:24
  51.2 20.6 %copy-start.1 = (bf16[3,3]{1,0:T(4,128)(2,1)S(1)}, bf16[3,3]{1,0:T(4,128)(2,1)}, u32[]{:S(2)}) copy-start(bf16[3,3]{1,0:T(4,128)(2,1)} %param.10) | copy-start | bytes 58
  51.2 21.3 %copy-start.2 = (bf16[3,3]{1,0:T(4,128)(2,1)S(1)}, bf16[3,3]{1,0:T(4,128)(2,1)}, u32[]{:S(2)}) copy-start(bf16[3,3]{1,0:T(4,128)(2,1)} %param.11) | copy-start | bytes 58
  51.7 47.3 %collective-permute-start.4 = (bf16[16,1,256,256]{3,2,0,1:T(8,128)(2,1)S(1)}, bf16[16,1,256,256]{3,2,0,1:T(8,128)(2,1)}, u32[]{:S(2)}, u32[]{:S(2)}) collective-permute-start(bf16[16,1,256,256]{3,2,0,1:T(8,128)(2,1)S(1)} %bitcast.152), channel_id=1, source_target_pairs={{0,16},{1,17},{2,18},{3,19},{4,20},{5,21},{6,22},{7,23},{8,24},{9,... | collective-permute-start | bytes 6291464 | tf_op jit(solution)/shard_map/ppermute | solution.py:24
  66.8 32.2 %all-to-all-start = ((s32[2,32,8]{2,0,1:T(2,128)}), s32[2,32,8]{2,0,1:T(2,128)S(1)}, u32[]{:S(2)}, u32[]{:S(2)}) async-start(s32[2,32,8]{2,0,1:T(2,128)} %copy.26), calls=%async_computation | async-start | bytes 65536 | tf_op jit(solution)/shard_map/all_to_all | solution.py:117
  71.8 4.5 %copy-start = (bf16[32,256,256]{2,1,0:T(8,128)(2,1)S(1)}, bf16[32,256,256]{2,1,0:T(8,128)(2,1)}, u32[]{:S(2)}) copy-start(bf16[32,256,256]{2,1,0:T(8,128)(2,1)} %param.8) | copy-start | bytes 12582916
  338.3 2.7 copy-start.4
